TPU v7x, 32 devices: a whole 2x2x4 slice. The times are simulated.
32 devices in a mesh: groups: 2 (over y), cells: 4 (over z), freq: 2 (over x), rep: 2 (over core).
Axes of the slice: x: 2, y: 2, z: 4, core: 2. Of those that a mesh axis runs over, the one named last changes fastest.
Arguments:
- far_adjoint: bfloat16 [16, 128, 2, 128], P(('groups', 'freq'), 'cells'), parts along dimension 0, may hold values from -6 to 6
- wavenumber: float32 [8], P('freq'), may hold values from 0.6 to 2.4
- design_params: bfloat16 [8, 131072], P(None, ('groups', 'cells', 'freq', 'rep')), parts along dimension 1, may hold values from -5 to 5
- family: int32 [256, 512], P(('groups', 'cells'), 'rep'), parts along dimension 0, may hold values from 0 to 7, as said below
- send_pick: int32 [16, 8, 1536], P(('groups', 'cells', 'rep')), parts along dimension 0, may hold values from 0 to 8192, as said below
- arrive_pick: int32 [16, 8192], P(('groups', 'cells', 'rep')), parts along dimension 0, may hold values from 0 to 12287, as said below
- input_weight: bfloat16 [8, 256, 8], replicated, may hold values from -2 to 2
- hidden_weight: bfloat16 [8, 5, 256, 256], replicated, may hold values from -0.5 to 0.5
- output_weight: bfloat16 [8, 16, 256], replicated, may hold values from -1.5 to 1.5
Outputs:
- design_gradient: float32 [8, 131072], P(None, ('groups', 'cells', 'freq', 'rep')), parts along dimension 1
There are 2 independent parts, one for each index of `groups`. A program takes and returns all parts, laid end to end along the dimension named above; an argument that names none is the same for every part. Nothing has to cross between parts.
Inputs may be any that keep to these rules, and one draw needn't show every extreme that they name: send_pick[s, g, k] is the cell a * 256 + b (surface row (s // 2) * 32 + a, column (s % 2) * 256 + b) of surface block s that fills slot k towards sorted block g, or 8192 for an empty slot; used slots come first; every cell is sent exactly once; some pair of blocks uses all 1536 slots in every draw; every sorted block receives exactly 8192 cells. arrive_pick[g, t] = s * 1536 + k names the used slot k from surface block s towards sorted block g; each used slot is named exactly once. Along the family-sorted order families never decrease, every aligned block of 128 positions holds cells of one family, and every family occurs.
All inputs are finite; a program needn't handle non-finite values.
Results may differ from a plain program's by a relative error of at most 0.011.
Values may be sent and summed in bfloat16 or wider, within the bound.
A program may use at most 128 MiB of HBM per device.

v0:
```python
import functools
import math

import jax
import jax.numpy as jnp
from jax import lax
from jax.experimental import pallas as pl
from jax.experimental.pallas import tpu as pltpu
from jax.sharding import PartitionSpec as P

U = 128
V = 128
HID = 256
NL = 5
BLK = 128
NFAM = 8
SUB = 8
TILE = 1024
PAIR = 4


def one_hot_pick(table, index, width):
    count = index.shape[1]
    low = jnp.bitwise_and(index, width - 1).astype(jnp.float32).astype(jnp.bfloat16)
    high = jnp.right_shift(index, width.bit_length() - 1)
    level = lax.broadcasted_iota(jnp.int32, (width, count), 0)
    level = level.astype(jnp.float32).astype(jnp.bfloat16)
    one, zero = jnp.ones((), jnp.bfloat16), jnp.zeros((), jnp.bfloat16)
    chosen = jnp.where(level == jnp.broadcast_to(low, level.shape), one, zero)
    spread = jnp.dot(table, chosen, preferred_element_type=jnp.float32)
    high = jnp.broadcast_to(high, (SUB, count))
    total = jnp.zeros((SUB, count), jnp.float32)
    for step in range(table.shape[0] // SUB):
        total = jnp.where(high == step, spread[step * SUB : (step + 1) * SUB], total)
    return total


def row_order(pair_rows, row_count):
    shape = (row_count * SUB, pair_rows * row_count)
    target = lax.broadcasted_iota(jnp.int32, shape, 0)
    source = lax.broadcasted_iota(jnp.int32, shape, 1)
    wanted = (target % SUB) * row_count + target // SUB
    hit = jnp.logical_and(wanted == source, target % SUB < pair_rows)
    return jnp.where(hit, 1.0, 0.0).astype(jnp.bfloat16)


def angles_of(wavenumber, direction, position):
    return (wavenumber * direction) * position


def fill_right_tables(right_ref, wave_ref, column_start, column_count, column_total):
    group = 16
    scale = 1.0 / math.sqrt(V)
    for band in range(right_ref.shape[0]):
        wavenumber = wave_ref[band]
        for start in range(0, column_count, 128):
            column = lax.broadcasted_iota(jnp.int32, (group, 128), 1) + (column_start + start)
            position = column.astype(jnp.float32) - 0.5 * (column_total - 1)
            row = lax.broadcasted_iota(jnp.int32, (group, 128), 0).astype(jnp.float32)
            angle = angles_of(wavenumber, (2.0 * row + 1.0) / V - 1.0, position)
            cosine, sine = jnp.cos(angle) * scale, jnp.sin(angle) * scale
            turn = angles_of(wavenumber, 2.0 * group / V, position[:8])
            turn_cos, turn_sin = jnp.cos(turn), jnp.sin(turn)
            turn_cos = jnp.concatenate([turn_cos, turn_cos], 0)
            turn_sin = jnp.concatenate([turn_sin, turn_sin], 0)
            for low in range(0, V, group):
                up, down = pl.ds(low, group), pl.ds(V + low, group)
                real, imag = pl.ds(start, 128), pl.ds(column_count + start, 128)
                right_ref[band, up, real] = cosine.astype(jnp.bfloat16)
                right_ref[band, up, imag] = sine.astype(jnp.bfloat16)
                right_ref[band, down, real] = (-sine).astype(jnp.bfloat16)
                right_ref[band, down, imag] = cosine.astype(jnp.bfloat16)
                cosine, sine = (
                    cosine * turn_cos - sine * turn_sin,
                    sine * turn_cos + cosine * turn_sin,
                )


def fill_left_tables(left_ref, wave_ref, row_start, row_count, rows_total):
    scale = 1.0 / math.sqrt(U)
    row = lax.broadcasted_iota(jnp.int32, (row_count, U), 0) + row_start
    position = row.astype(jnp.float32) - 0.5 * (rows_total - 1)
    lane = lax.broadcasted_iota(jnp.int32, (row_count, U), 1).astype(jnp.float32)
    direction = (2.0 * lane + 1.0) / U - 1.0
    for band in range(left_ref.shape[0]):
        angle = angles_of(wave_ref[band], direction, position)
        cosine = (jnp.cos(angle) * scale).astype(jnp.bfloat16)
        sine = (jnp.sin(angle) * scale).astype(jnp.bfloat16)
        left_ref[band, :row_count, :U] = cosine
        left_ref[band, :row_count, U:] = -sine
        left_ref[band, row_count:, :U] = sine
        left_ref[band, row_count:, U:] = cosine


def exchange_kernel(
    wave_hbm,
    far_ref,
    family_hbm,
    send_hbm,
    arrive_hbm,
    ordered_ref,
    kind_ref,
    wave_ref,
    family_ref,
    send_ref,
    arrive_ref,
    load_sem,
    field_ref,
    right_ref,
    left_ref,
    cells_ref,
    table_ref,
    out_ref,
    got_ref,
    gather_ref,
    half_ref,
    count_ref,
    counts_ref,
    far_send,
    far_recv,
    pass_send,
    pass_recv,
    count_send,
    count_recv,
    out_send,
    out_recv,
    half_send,
    half_recv,
    *,
    width,
):
    n_cells, n_rep, n_freq = (lax.axis_size(name) for name in ("cells", "rep", "freq"))
    z, core, freq = (lax.axis_index(name) for name in ("cells", "rep", "freq"))
    shards = n_cells * n_rep
    me = z * n_rep + core
    bands = far_ref.shape[0]
    row_count, column_count = family_ref.shape
    slots = send_ref.shape[1]
    segment = ordered_ref.shape[1]
    pair_rows = 2 * bands
    share = bands // n_rep
    mesh_ids = pl.DeviceIdType.MESH

    def shard_id(shard):
        return {"cells": shard // n_rep, "rep": shard % n_rep}

    loads = [
        pltpu.make_async_copy(source, target, load_sem.at[place])
        for place, (source, target) in enumerate(
            (
                (wave_hbm, wave_ref),
                (family_hbm, family_ref),
                (send_hbm, send_ref),
                (arrive_hbm, arrive_ref),
                (far_ref, field_ref.at[z]),
            )
        )
    ]
    for load in loads:
        load.start()

    barrier = pltpu.get_barrier_semaphore()

    @pl.loop(1, shards)
    def _(step):
        pl.semaphore_signal(
            barrier, inc=1, device_id=shard_id((me + step) % shards), device_id_type=mesh_ids
        )

    @pl.loop(1, n_freq)
    def _(step):
        pl.semaphore_signal(
            barrier, inc=1, device_id={"freq": (freq + step) % n_freq}, device_id_type=mesh_ids
        )

    pl.semaphore_wait(barrier, shards - 1 + n_freq - 1)

    def far_copy(step):
        mine = pl.ds(core * share, share)
        target = (z + step) % n_cells
        return pltpu.make_async_remote_copy(
            src_ref=far_ref.at[mine],
            dst_ref=field_ref.at[z, mine],
            send_sem=far_send.at[step],
            recv_sem=far_recv.at[step],
            device_id={"cells": target},
            device_id_type=mesh_ids,
        )

    def far_arrival(step):
        mine = pl.ds(core * share, share)
        source = (z - step + n_cells) % n_cells
        return pltpu.make_async_remote_copy(
            src_ref=far_ref.at[mine],
            dst_ref=field_ref.at[source, mine],
            send_sem=far_send.at[step],
            recv_sem=far_recv.at[step],
            device_id={"cells": source},
            device_id_type=mesh_ids,
        )

    def pass_copy(step, lane):
        mine = pl.ds(lane * share, share)
        source = (z - step + n_cells) % n_cells
        return pltpu.make_async_remote_copy(
            src_ref=field_ref.at[source, mine],
            dst_ref=field_ref.at[source, mine],
            send_sem=pass_send.at[step],
            recv_sem=pass_recv.at[step],
            device_id={"rep": 1 - core},
            device_id_type=mesh_ids,
        )

    for step in range(1, n_cells):
        far_copy(step).start()
    for load in loads:
        load.wait()

    rows = []
    for kind in range(NFAM):
        below = jnp.where(family_ref[...] <= kind, 1.0, 0.0)
        part = jnp.sum(below, 0, keepdims=True)
        total = part[:, :128]
        for start in range(128, column_count, 128):
            total = total + part[:, start : start + 128]
        rows.append(total)
    count_ref[...] = jnp.concatenate(rows, 0)
    counts_ref[me] = count_ref[...]

    def count_copy(step, shard, slot):
        return pltpu.make_async_remote_copy(
            src_ref=count_ref,
            dst_ref=counts_ref.at[slot],
            send_sem=count_send.at[step],
            recv_sem=count_recv.at[slot],
            device_id=shard_id(shard),
            device_id_type=mesh_ids,
        )

    @pl.loop(1, shards)
    def _(step):
        count_copy(step, (me + step) % shards, me).start()

    fill_right_tables(right_ref, wave_ref, core * column_count, column_count, column_count * n_rep)
    fill_left_tables(left_ref, wave_ref, z * row_count, row_count, row_count * n_cells)

    for step in range(1, n_cells):
        far_arrival(step).wait_recv()
        pass_copy(step, core).start()
    for step in range(1, n_cells):
        pass_copy(step, 1 - core).wait_recv()

    for band in range(bands):
        field = field_ref[:, band].astype(jnp.float32).reshape(U, 2 * V).astype(jnp.bfloat16)
        image = jnp.dot(field, right_ref[band], preferred_element_type=jnp.float32).astype(
            jnp.bfloat16
        )
        stacked = jnp.concatenate([image[:, :column_count], image[:, column_count:]], 0)
        cells_ref[band * 2 * row_count : (band + 1) * 2 * row_count] = jnp.dot(
            left_ref[band], stacked, preferred_element_type=jnp.float32
        ).astype(jnp.bfloat16)
    table_ref[...] = jnp.dot(
        row_order(pair_rows, row_count), cells_ref[...], preferred_element_type=jnp.float32
    ).astype(jnp.bfloat16)

    def out_copy(shard, slot):
        return pltpu.make_async_remote_copy(
            src_ref=out_ref.at[shard],
            dst_ref=got_ref.at[slot],
            send_sem=out_send.at[shard],
            recv_sem=out_recv.at[slot],
            device_id=shard_id(shard),
            device_id_type=mesh_ids,
        )

    chunk = 384

    def partner(mask):
        other, bit = 0, 1
        while bit < shards:
            mine, flip = (me // bit) % 2, (mask // bit) % 2
            other, bit = other + bit * (mine + flip - 2 * mine * flip), 2 * bit
        return other

    @pl.loop(1, shards)
    def _(step):
        shard = partner(shards - step)
        for start in range(0, slots, chunk):
            at = pl.ds(start, chunk)
            picked = one_hot_pick(table_ref[...], send_ref[pl.ds(shard, 1), at], column_count)
            out_ref[shard, :, at] = picked.astype(jnp.bfloat16)
        out_copy(shard, me).start()

    for start in range(0, slots, chunk):
        at = pl.ds(start, chunk)
        picked = one_hot_pick(table_ref[...], send_ref[pl.ds(me, 1), at], column_count)
        got_ref[me, :, at] = picked.astype(jnp.bfloat16)

    @pl.loop(1, shards)
    def _(step):
        count_copy(step, (me + step) % shards, (me + step) % shards).wait_recv()

    upto = jnp.sum(jnp.sum(counts_ref[...], 0), 1, keepdims=True)
    owner = (z * n_freq + freq) * n_rep + core
    block = lax.broadcasted_iota(jnp.int32, (NFAM, 128), 1)
    level = lax.broadcasted_iota(jnp.int32, (NFAM, 128), 0)
    position = (owner * segment + block * BLK).astype(jnp.float32)
    past = jnp.where(jnp.logical_and(position >= upto, level < NFAM - 1), 1.0, 0.0)
    kind_ref[...] = jnp.sum(past, 0, keepdims=True).astype(jnp.int32)

    @pl.loop(1, shards)
    def _(step):
        shard = (me + step) % shards
        out_copy(shard, shard).wait_recv()

    per_shard = slots // width
    for shard in range(shards):
        for part in range(per_shard):
            row = (shard * per_shard + part) * SUB
            gather_ref[row : row + SUB] = got_ref[
                shard, :, part * width : (part + 1) * width
            ].astype(jnp.float32)
    gathered = gather_ref[...].astype(jnp.bfloat16)

    def half_copy(step, slot):
        return pltpu.make_async_remote_copy(
            src_ref=half_ref.at[0, step],
            dst_ref=half_ref.at[1, slot],
            send_sem=half_send.at[step],
            recv_sem=half_recv.at[slot],
            device_id={"freq": (freq + step) % n_freq},
            device_id_type=mesh_ids,
        )

    piece = 512

    @pl.loop(1, n_freq)
    def _(step):
        target = (freq + step) % n_freq
        for start in range(0, segment, piece):
            at = pl.ds(pl.multiple_of(target * segment + start, piece), piece)
            half_ref[0, step, :, pl.ds(start, piece)] = one_hot_pick(
                gathered, arrive_ref[:, at], width
            ).astype(jnp.bfloat16)
        half_copy(step, freq).start()

    for start in range(0, segment, piece):
        at = pl.ds(pl.multiple_of(freq * segment + start, piece), piece)
        half_ref[1, freq, :, pl.ds(start, piece)] = one_hot_pick(
            gathered, arrive_ref[:, at], width
        ).astype(jnp.bfloat16)

    @pl.loop(1, n_freq)
    def _(step):
        half_copy(step, (freq + step) % n_freq).wait_recv()

    for group in range(n_freq):
        ordered_ref[group * SUB : (group + 1) * SUB] = half_ref[1, group]

    for step in range(1, n_cells):
        far_copy(step).wait_send()
        pass_copy(step, core).wait_send()

    @pl.loop(1, shards)
    def _(step):
        count_copy(step, (me + step) % shards, me).wait_send()
        out_copy((me + step) % shards, me).wait_send()

    @pl.loop(1, n_freq)
    def _(step):
        half_copy(step, freq).wait_send()


def nt_dot(left, right):
    return lax.dot_general(
        left, right, (((1,), (1,)), ((), ())), preferred_element_type=jnp.float32
    )


def tn_dot(left, right):
    return lax.dot_general(
        left, right, (((0,), (0,)), ((), ())), preferred_element_type=jnp.float32
    )


def network(parts, first_ref, hidden_ref, last_ref, above_ref, active_ref):
    half = jnp.asarray(0.5, jnp.bfloat16)

    offsets = [0]
    for inputs, _, _ in parts:
        offsets.append(offsets[-1] + inputs.shape[1])

    def slope_of(level, place):
        rows = slice(offsets[place], offsets[place + 1])
        above = above_ref[level, rows]
        return above + active_ref[level, rows] * (2.0 - above)

    preacts = [tn_dot(inputs * half, first_ref[kind]) for inputs, _, kind in parts]
    for level in range(NL + 1):
        for place, (_, _, kind) in enumerate(parts):
            above = 1.0 + jnp.tanh(preacts[place])
            activation = preacts[place] * above
            rows = slice(offsets[place], offsets[place + 1])
            above_ref[level, rows] = above
            active_ref[level, rows] = activation
            if level < NL:
                preacts[place] = nt_dot(
                    activation.astype(jnp.bfloat16) * half, hidden_ref[kind, level]
                )
    gradients = [tn_dot(adjoint, last_ref[kind]) for _, adjoint, kind in parts]
    for level in reversed(range(NL)):
        for place, (_, _, kind) in enumerate(parts):
            delta = (gradients[place] * slope_of(level + 1, place)).astype(jnp.bfloat16)
            gradients[place] = jnp.dot(
                delta, hidden_ref[kind, level], preferred_element_type=jnp.float32
            )
    return [
        nt_dot(
            first_ref[kind], (gradients[place] * slope_of(0, place)).astype(jnp.bfloat16)
        )
        * (0.5 ** (NL + 1))
        for place, (_, _, kind) in enumerate(parts)
    ]


def network_kernel(
    kind_ref,
    adjoint_hbm,
    inputs_hbm,
    first_hbm,
    hidden_hbm,
    last_hbm,
    out_ref,
    adjoint_ref,
    inputs_ref,
    first_ref,
    hidden_ref,
    last_ref,
    above_ref,
    active_ref,
    sems,
    hidden_sems,
    *,
    tile,
):
    blocks = tile // BLK
    total = inputs_ref.shape[1] // BLK
    small = [
        pltpu.make_async_copy(source, target, sems.at[place])
        for place, (source, target) in enumerate(
            (
                (inputs_hbm, inputs_ref),
                (first_hbm, first_ref),
                (last_hbm, last_ref),
                (adjoint_hbm, adjoint_ref),
            )
        )
    ]
    for copy in small:
        copy.start()

    def family_copy(kind):
        return pltpu.make_async_copy(
            hidden_hbm.at[kind], hidden_ref.at[kind], hidden_sems.at[kind]
        )

    lowest, highest = kind_ref[0], kind_ref[total - 1]

    @pl.loop(lowest, highest + 1)
    def _(kind):
        family_copy(kind).start()

    for copy in small:
        copy.wait()

    def tile_step(step, ready):
        first_block = step * blocks
        kind = kind_ref[first_block]
        last = kind_ref[first_block + blocks - 1]

        @pl.loop(ready, last + 1)
        def _(kind):
            family_copy(kind).wait()

        def run(pieces):
            where = [pl.ds(pl.multiple_of(start, BLK), size) for start, size, _ in pieces]
            parts = [
                (inputs_ref[:, at], adjoint_ref[:, at], kind)
                for at, (_, _, kind) in zip(where, pieces)
            ]
            for at, result in zip(where, network(parts, first_ref, hidden_ref, last_ref, above_ref, active_ref)):
                out_ref[:, at] = result

        @pl.when(kind == last)
        def _():
            run([(step * tile, tile, kind)])

        @pl.when(kind != last)
        def _():
            @pl.loop(0, blocks // PAIR)
            def _(pair):
                first = first_block + pair * PAIR
                run([((first + i) * BLK, BLK, kind_ref[first + i]) for i in range(PAIR)])

        return last + 1

    lax.fori_loop(0, total // blocks, tile_step, lowest)


def vmem(count):
    return [pl.BlockSpec(memory_space=pltpu.VMEM)] * count


def far_memory(count):
    return [pl.BlockSpec(memory_space=pltpu.HBM)] * count


def run_network(block_kind, inputs, adjoint, input_weight, hidden_weight, output_weight):
    tile = min(TILE, inputs.shape[1])
    input_weight = jnp.swapaxes(input_weight, 1, 2)
    operands = (adjoint, inputs, input_weight, hidden_weight, output_weight)
    return pl.pallas_call(
        functools.partial(network_kernel, tile=tile),
        out_shape=jax.ShapeDtypeStruct(inputs.shape, jnp.float32),
        in_specs=[pl.BlockSpec(memory_space=pltpu.SMEM)] + far_memory(5),
        out_specs=pl.BlockSpec(memory_space=pltpu.VMEM),
        scratch_shapes=[pltpu.VMEM(item.shape, item.dtype) for item in operands]
        + [pltpu.VMEM((NL + 1, tile, HID), jnp.float32)] * 2
        + [pltpu.SemaphoreType.DMA((4,)), pltpu.SemaphoreType.DMA((NFAM,))],
        compiler_params=pltpu.CompilerParams(vmem_limit_bytes=62 << 20),
        name="network",
    )(block_kind, *operands)


def per_device(
    far_adjoint,
    wavenumber,
    design_params,
    family,
    send_pick,
    arrive_pick,
    input_weight,
    hidden_weight,
    output_weight,
):
    row_count, column_count = family.shape
    cell_count = row_count * column_count
    bands = far_adjoint.shape[0]
    band_groups = lax.axis_size("freq")
    segment = cell_count // band_groups
    pair_rows = 2 * bands
    shards, slots = send_pick.shape[1:]
    directions = far_adjoint.shape[1]
    n_cells = lax.axis_size("cells")
    width = 256 if slots % 256 == 0 else 128
    bf16, dma = jnp.bfloat16, pltpu.SemaphoreType.DMA
    ordered, block_kind = pl.pallas_call(
        functools.partial(exchange_kernel, width=width),
        out_shape=(
            jax.ShapeDtypeStruct((band_groups * SUB, segment), bf16),
            jax.ShapeDtypeStruct((1, 128), jnp.int32),
        ),
        in_specs=far_memory(5),
        out_specs=tuple(vmem(2)),
        scratch_shapes=[
            pltpu.SMEM(wavenumber.shape, jnp.float32),
            pltpu.VMEM(family.shape, jnp.int32),
            pltpu.VMEM((shards, slots), jnp.int32),
            pltpu.VMEM(arrive_pick.shape, jnp.int32),
            dma((5,)),
            pltpu.VMEM((n_cells, bands, directions, 2 * V), bf16),
            pltpu.VMEM((bands, 2 * V, 2 * column_count), bf16),
            pltpu.VMEM((bands, 2 * row_count, 2 * U), bf16),
            pltpu.VMEM((pair_rows * row_count, column_count), bf16),
            pltpu.VMEM((row_count * SUB, column_count), bf16),
            pltpu.VMEM((shards, SUB, slots), bf16),
            pltpu.VMEM((shards, SUB, slots), bf16),
            pltpu.VMEM((shards * slots // width * SUB, width), jnp.float32),
            pltpu.VMEM((2, band_groups, SUB, segment), bf16),
            pltpu.VMEM((NFAM, 128), jnp.float32),
            pltpu.VMEM((shards, NFAM, 128), jnp.float32),
            dma((n_cells,)),
            dma((n_cells,)),
            dma((n_cells,)),
            dma((n_cells,)),
            dma((shards,)),
            dma((shards,)),
            dma((shards,)),
            dma((shards,)),
            dma((band_groups,)),
            dma((band_groups,)),
        ],
        compiler_params=pltpu.CompilerParams(
            collective_id=0, has_side_effects=True, vmem_limit_bytes=62 << 20
        ),
        name="exchange",
    )(
        wavenumber,
        far_adjoint.reshape(bands, directions, 2 * V),
        family,
        send_pick.reshape(shards, slots),
        arrive_pick,
    )
    last_weight = output_weight.reshape(NFAM, band_groups, pair_rows, HID)
    last_weight = jnp.pad(last_weight, ((0, 0), (0, 0), (0, SUB - pair_rows), (0, 0)))
    return run_network(
        block_kind.reshape(128),
        design_params,
        ordered,
        input_weight,
        hidden_weight,
        last_weight.reshape(NFAM, band_groups * SUB, HID),
    )


def solution(mesh):
    return jax.shard_map(
        per_device,
        mesh=mesh,
        in_specs=(
            P(("groups", "freq"), "cells", None, None),
            P("freq"),
            P(None, ("groups", "cells", "freq", "rep")),
            P(("groups", "cells"), "rep"),
            P(("groups", "cells", "rep"), None, None),
            P(("groups", "cells", "rep"), None),
            P(),
            P(),
            P(),
        ),
        out_specs=P(None, ("groups", "cells", "freq", "rep")),
        check_vma=False,
    )
```

profile of v0, /device:TPU:0, one launch (start us, length us, event | category | flops | bytes accessed | tf_op | source)
XLA Modules:
  0.0 37.4 jit_solution(3404779482535902913)
XLA Ops:
  0.0 1.5 %reshape.11.far_ref = bf16[4,32,256]{2,1,0:T(8,128)(2,1)} reshape(bf16[4,32,2,128]{3,2,1,0:T(2,128)(2,1)} %param.9) | data formatting | bytes 131072 | tf_op jit(solution)/shard_map/reshape | solution.py:599
  1.5 24.5 %exchange.1 = (bf16[16,4096]{1,0:T(8,128)(2,1)}, s32[1,128]{1,0:T(1,128)}) custom-call(f32[4]{0:T(128)} %wave_hbm.1, bf16[4,32,256]{2,1,0:T(8,128)(2,1)} %reshape.11.far_ref, s32[32,256]{1,0:T(8,128)} %family_hbm.1, s32[8,1536]{1,0:T(8,128)} %bitcast.3, s32[1,8192]{1,0:T(1,128)} %arrive_hbm.1), custom_call_target="tpu_custom_call" | custom-call | tf_op jit(solution)/shard_map/exchange/pallas_call | solution.py:557
  26.0 11.3 %network.1 = f32[8,4096]{1,0:T(8,128)} custom-call(s32[128]{0:T(128)} %bitcast.5, bf16[16,4096]{1,0:T(8,128)(2,1)} %get-tuple-element.8.adjoint_hbm, bf16[8,4096]{1,0:T(8,128)(2,1)} %inputs_hbm.1, bf16[8,8,256]{2,1,0:T(8,128)(2,1)} %bitcast.4, bf16[8,5,256,256]{3,2,1,0:T(8,128)(2,1)} %hidden_hbm.1, bf16[8,16,256]{2,1,0:T(8,128)(2,1)} %last_hbm.1), custom_call_target="tpu_custom_call" | custom-call | tf_op jit(solution)/shard_map/network/pallas_call | solution.py:522
where the time goes:
time: 37.6 us; the launch traced here: 37.4 us
  Pallas kernels  35.9 us (95%)
  local copies, waits for them, and re-layouts  1.51 us (4%)
    pallas_call x1, Pallas kernels, per_device(): pl.pallas_call(functools.partial(exchange_kernel, width=width), out_shape...  24.5 us
    pallas_call x1, Pallas kernels, run_network(): pl.pallas_call(functools.partial(network_kernel, tile=tile), out_shape=ja...  11.3 us
    reshape x1, local copies, waits for them, and re-layouts, per_device(): far_adjoint.reshape(bands, directions, 2 * V)  1.51 us

commit v1 on v0

v1 whole, which is shorter than its diff:
```python
import functools
import math

import jax
import jax.numpy as jnp
from jax import lax
from jax.experimental import pallas as pl
from jax.experimental.pallas import tpu as pltpu
from jax.sharding import PartitionSpec as P

U = 128
V = 128
HID = 256
NL = 5
BLK = 128
NFAM = 8
SUB = 8
CHUNK = 1024
LATE = 1


def one_hot_pick(table, index, width):
    count = index.shape[1]
    low = jnp.bitwise_and(index, width - 1).astype(jnp.float32).astype(jnp.bfloat16)
    high = jnp.right_shift(index, width.bit_length() - 1)
    level = lax.broadcasted_iota(jnp.int32, (width, count), 0)
    level = level.astype(jnp.float32).astype(jnp.bfloat16)
    one, zero = jnp.ones((), jnp.bfloat16), jnp.zeros((), jnp.bfloat16)
    chosen = jnp.where(level == jnp.broadcast_to(low, level.shape), one, zero)
    spread = jnp.dot(table, chosen, preferred_element_type=jnp.float32)
    high = jnp.broadcast_to(high, (SUB, count))
    total = jnp.zeros((SUB, count), jnp.float32)
    for step in range(table.shape[0] // SUB):
        total = jnp.where(high == step, spread[step * SUB : (step + 1) * SUB], total)
    return total


def row_order(pair_rows, row_count):
    shape = (row_count * SUB, pair_rows * row_count)
    target = lax.broadcasted_iota(jnp.int32, shape, 0)
    source = lax.broadcasted_iota(jnp.int32, shape, 1)
    wanted = (target % SUB) * row_count + target // SUB
    hit = jnp.logical_and(wanted == source, target % SUB < pair_rows)
    return jnp.where(hit, 1.0, 0.0).astype(jnp.bfloat16)


def angles_of(wavenumber, direction, position):
    return (wavenumber * direction) * position


def fill_right_tables(right_ref, wave_ref, column_start, column_count, column_total):
    group = 16
    scale = 1.0 / math.sqrt(V)
    for band in range(right_ref.shape[0]):
        wavenumber = wave_ref[band]
        for start in range(0, column_count, 128):
            column = lax.broadcasted_iota(jnp.int32, (group, 128), 1) + (column_start + start)
            position = column.astype(jnp.float32) - 0.5 * (column_total - 1)
            row = lax.broadcasted_iota(jnp.int32, (group, 128), 0).astype(jnp.float32)
            angle = angles_of(wavenumber, (2.0 * row + 1.0) / V - 1.0, position)
            cosine, sine = jnp.cos(angle) * scale, jnp.sin(angle) * scale
            turn = angles_of(wavenumber, 2.0 * group / V, position[:8])
            turn_cos, turn_sin = jnp.cos(turn), jnp.sin(turn)
            turn_cos = jnp.concatenate([turn_cos, turn_cos], 0)
            turn_sin = jnp.concatenate([turn_sin, turn_sin], 0)
            for low in range(0, V, group):
                at = pl.ds(low, group)
                right_ref[band, at, pl.ds(start, 128)] = cosine.astype(jnp.bfloat16)
                right_ref[band, at, pl.ds(column_count + start, 128)] = sine.astype(jnp.bfloat16)
                cosine, sine = (
                    cosine * turn_cos - sine * turn_sin,
                    sine * turn_cos + cosine * turn_sin,
                )


def fill_left_tables(left_ref, wave_ref, row_start, row_count, rows_total):
    scale = 1.0 / math.sqrt(U)
    shape = (row_count, 2 * U)
    row = lax.broadcasted_iota(jnp.int32, shape, 0) + row_start
    position = row.astype(jnp.float32) - 0.5 * (rows_total - 1)
    lane = lax.broadcasted_iota(jnp.int32, shape, 1)
    direction = (2.0 * (lane // 2).astype(jnp.float32) + 1.0) / U - 1.0
    real = lane % 2 == 0
    for band in range(left_ref.shape[0]):
        angle = angles_of(wave_ref[band], direction, position)
        cosine, sine = jnp.cos(angle) * scale, jnp.sin(angle) * scale
        upper = jnp.where(real, cosine, -sine).astype(jnp.bfloat16)
        lower = jnp.where(real, sine, cosine).astype(jnp.bfloat16)
        left_ref[band, :row_count, : 2 * U] = upper
        left_ref[band, row_count:, : 2 * U] = lower
        left_ref[band, :row_count, 2 * U :] = -lower
        left_ref[band, row_count:, 2 * U :] = upper


def nt_dot(left, right):
    return lax.dot_general(
        left, right, (((1,), (1,)), ((), ())), preferred_element_type=jnp.float32
    )


def tn_dot(left, right):
    return lax.dot_general(
        left, right, (((0,), (0,)), ((), ())), preferred_element_type=jnp.float32
    )


def blocks_of(chunk, kind_ref):
    first = chunk * (CHUNK // BLK)
    return [
        (
            pl.ds(pl.multiple_of((first + i) * BLK, BLK), BLK),
            jnp.clip(kind_ref[0, first + i], 0, NFAM - 1),
        )
        for i in range(CHUNK // BLK)
    ]


def forward_chunk(chunk, kind_ref, inputs_ref, first_ref, hidden_ref, slope_ref):
    half = jnp.asarray(0.5, jnp.bfloat16)
    blocks = blocks_of(chunk, kind_ref)
    preacts = [tn_dot(inputs_ref[:, at] * half, first_ref[kind]) for at, kind in blocks]
    for level in range(NL + 1):
        for place, (at, kind) in enumerate(blocks):
            above = 1.0 + jnp.tanh(preacts[place])
            active = preacts[place] * above
            slope_ref[level, at] = (above + active * (2.0 - above)).astype(jnp.bfloat16)
            if level < NL:
                preacts[place] = nt_dot(active.astype(jnp.bfloat16) * half, hidden_ref[kind, level])


def backward_chunk(chunk, kind_ref, ordered_ref, first_ref, hidden_ref, last_ref, slope_ref, out_ref):
    blocks = blocks_of(chunk, kind_ref)

    def delta_of(level, place, at):
        slope = slope_ref[level, at].astype(jnp.float32)
        return (gradients[place] * slope).astype(jnp.bfloat16)

    gradients = [tn_dot(ordered_ref[:, at], last_ref[kind]) for at, kind in blocks]
    for level in reversed(range(NL)):
        for place, (at, kind) in enumerate(blocks):
            gradients[place] = jnp.dot(
                delta_of(level + 1, place, at),
                hidden_ref[kind, level],
                preferred_element_type=jnp.float32,
            )
    for place, (at, kind) in enumerate(blocks):
        out_ref[:, at] = nt_dot(first_ref[kind], delta_of(0, place, at)) * (0.5 ** (NL + 1))


def fused_kernel(
    wave_hbm,
    far_ref,
    family_hbm,
    send_hbm,
    arrive_hbm,
    inputs_hbm,
    first_hbm,
    hidden_hbm,
    last_hbm,
    out_hbm,
    wave_ref,
    family_ref,
    send_ref,
    arrive_ref,
    inputs_ref,
    first_ref,
    hidden_ref,
    last_ref,
    load_sem,
    field_ref,
    right_ref,
    left_ref,
    cells_ref,
    table_ref,
    outbox_ref,
    got_ref,
    gather_ref,
    half_ref,
    ordered_ref,
    count_ref,
    counts_ref,
    kind_vmem,
    kind_ref,
    slope_ref,
    result_ref,
    far_send,
    far_recv,
    pass_send,
    pass_recv,
    count_send,
    count_recv,
    out_send,
    out_recv,
    half_send,
    half_recv,
    result_sem,
    *,
    width,
):
    n_cells, n_rep, n_freq = (lax.axis_size(name) for name in ("cells", "rep", "freq"))
    z, core, freq = (lax.axis_index(name) for name in ("cells", "rep", "freq"))
    shards = n_cells * n_rep
    me = z * n_rep + core
    bands = far_ref.shape[0]
    row_count, column_count = family_ref.shape
    slots = send_ref.shape[1]
    segment = ordered_ref.shape[1]
    pair_rows = 2 * bands
    share = bands // n_rep
    chunks = segment // CHUNK
    mesh_ids = pl.DeviceIdType.MESH

    def shard_id(shard):
        return {"cells": shard // n_rep, "rep": shard % n_rep}

    def partner(own, mask, count):
        other, bit = 0, 1
        while bit < count:
            mine, flip = (own // bit) % 2, (mask // bit) % 2
            other, bit = other + bit * (mine + flip - 2 * mine * flip), 2 * bit
        return other

    loads = [
        pltpu.make_async_copy(source, target, load_sem.at[place])
        for place, (source, target) in enumerate(
            (
                (wave_hbm, wave_ref),
                (family_hbm, family_ref),
                (far_ref, field_ref.at[z]),
                (send_hbm, send_ref),
                (inputs_hbm, inputs_ref),
                (first_hbm, first_ref),
                (hidden_hbm, hidden_ref),
                (last_hbm, last_ref),
                (arrive_hbm, arrive_ref),
            )
        )
    ]
    for load in loads[:2]:
        load.start()

    barrier = pltpu.get_barrier_semaphore()

    @pl.loop(1, shards)
    def _(step):
        pl.semaphore_signal(
            barrier, inc=1, device_id=shard_id((me + step) % shards), device_id_type=mesh_ids
        )

    @pl.loop(1, n_freq)
    def _(step):
        pl.semaphore_signal(
            barrier, inc=1, device_id={"freq": (freq + step) % n_freq}, device_id_type=mesh_ids
        )

    for load in loads[2:]:
        load.start()
    for load in loads[:2]:
        load.wait()

    rows = []
    for kind in range(NFAM):
        below = jnp.where(family_ref[...] <= kind, 1.0, 0.0)
        part = jnp.sum(below, 0, keepdims=True)
        total = part[:, :128]
        for start in range(128, column_count, 128):
            total = total + part[:, start : start + 128]
        rows.append(total)
    count_ref[...] = jnp.concatenate(rows, 0)
    counts_ref[me] = count_ref[...]

    pl.semaphore_wait(barrier, shards - 1 + n_freq - 1)

    def far_copy(mask):
        mine = pl.ds(core * share, share)
        return pltpu.make_async_remote_copy(
            src_ref=far_ref.at[mine],
            dst_ref=field_ref.at[z, mine],
            send_sem=far_send.at[mask],
            recv_sem=far_recv.at[mask],
            device_id={"cells": partner(z, mask, n_cells)},
            device_id_type=mesh_ids,
        )

    def far_arrival(mask):
        mine = pl.ds(core * share, share)
        source = partner(z, mask, n_cells)
        return pltpu.make_async_remote_copy(
            src_ref=far_ref.at[mine],
            dst_ref=field_ref.at[source, mine],
            send_sem=far_send.at[mask],
            recv_sem=far_recv.at[mask],
            device_id={"cells": source},
            device_id_type=mesh_ids,
        )

    def pass_copy(mask, lane):
        mine = pl.ds(lane * share, share)
        source = partner(z, mask, n_cells)
        return pltpu.make_async_remote_copy(
            src_ref=field_ref.at[source, mine],
            dst_ref=field_ref.at[source, mine],
            send_sem=pass_send.at[mask],
            recv_sem=pass_recv.at[mask],
            device_id={"rep": 1 - core},
            device_id_type=mesh_ids,
        )

    def count_copy(step, shard, slot):
        return pltpu.make_async_remote_copy(
            src_ref=count_ref,
            dst_ref=counts_ref.at[slot],
            send_sem=count_send.at[step],
            recv_sem=count_recv.at[slot],
            device_id=shard_id(shard),
            device_id_type=mesh_ids,
        )

    @pl.loop(1, shards)
    def _(step):
        count_copy(step, (me + step) % shards, me).start()

    for mask in reversed(range(1, n_cells)):
        far_copy(mask).start()

    fill_right_tables(right_ref, wave_ref, core * column_count, column_count, column_count * n_rep)
    fill_left_tables(left_ref, wave_ref, z * row_count, row_count, row_count * n_cells)

    for load in loads[2:]:
        load.wait()

    @pl.loop(1, shards)
    def _(step):
        count_copy(step, (me + step) % shards, (me + step) % shards).wait_recv()

    upto = jnp.sum(jnp.sum(counts_ref[...], 0), 1, keepdims=True)
    owner = (z * n_freq + freq) * n_rep + core
    block = lax.broadcasted_iota(jnp.int32, (NFAM, 128), 1)
    level = lax.broadcasted_iota(jnp.int32, (NFAM, 128), 0)
    position = (owner * segment + block * BLK).astype(jnp.float32)
    past = jnp.where(jnp.logical_and(position >= upto, level < NFAM - 1), 1.0, 0.0)
    kind_vmem[...] = jnp.sum(past, 0, keepdims=True).astype(jnp.int32)
    kind_load = pltpu.make_async_copy(kind_vmem, kind_ref, load_sem.at[len(loads)])
    kind_load.start()
    kind_load.wait()

    def forward(chunk):
        forward_chunk(chunk, kind_ref, inputs_ref, first_ref, hidden_ref, slope_ref)

    early = min(chunks - LATE, n_cells - 1)

    @pl.loop(1, early + 1)
    def _(mask):
        far_arrival(mask).wait_recv()
        pass_copy(mask, core).start()
        forward(mask - 1)

    for mask in range(early + 1, n_cells):
        far_arrival(mask).wait_recv()
        pass_copy(mask, core).start()
    for mask in range(1, n_cells):
        pass_copy(mask, 1 - core).wait_recv()

    for band in range(bands):
        field = field_ref[:, band].reshape(2 * U, V)
        image = jnp.dot(field, right_ref[band], preferred_element_type=jnp.float32).astype(
            jnp.bfloat16
        )
        stacked = jnp.concatenate([image[:, :column_count], image[:, column_count:]], 0)
        cells_ref[band * 2 * row_count : (band + 1) * 2 * row_count] = jnp.dot(
            left_ref[band], stacked, preferred_element_type=jnp.float32
        ).astype(jnp.bfloat16)
    table_ref[...] = jnp.dot(
        row_order(pair_rows, row_count), cells_ref[...], preferred_element_type=jnp.float32
    ).astype(jnp.bfloat16)

    def out_copy(shard, slot):
        return pltpu.make_async_remote_copy(
            src_ref=outbox_ref.at[shard],
            dst_ref=got_ref.at[slot],
            send_sem=out_send.at[shard],
            recv_sem=out_recv.at[slot],
            device_id=shard_id(shard),
            device_id_type=mesh_ids,
        )

    grain = 384

    @pl.loop(1, shards)
    def _(step):
        shard = partner(me, shards - step, shards)
        for start in range(0, slots, grain):
            at = pl.ds(start, grain)
            picked = one_hot_pick(table_ref[...], send_ref[pl.ds(shard, 1), at], column_count)
            outbox_ref[shard, :, at] = picked.astype(jnp.bfloat16)
        out_copy(shard, me).start()

    for start in range(0, slots, grain):
        at = pl.ds(start, grain)
        picked = one_hot_pick(table_ref[...], send_ref[pl.ds(me, 1), at], column_count)
        got_ref[me, :, at] = picked.astype(jnp.bfloat16)

    pl.loop(early, chunks)(forward)

    @pl.loop(1, shards)
    def _(step):
        shard = (me + step) % shards
        out_copy(shard, shard).wait_recv()

    per_shard = slots // width
    for shard in range(shards):
        for part in range(per_shard):
            row = (shard * per_shard + part) * SUB
            gather_ref[row : row + SUB] = got_ref[
                shard, :, part * width : (part + 1) * width
            ].astype(jnp.float32)
    gathered = gather_ref[...].astype(jnp.bfloat16)

    def half_copy(step, slot, chunk):
        at = pl.ds(pl.multiple_of(chunk * CHUNK, CHUNK), CHUNK)
        return pltpu.make_async_remote_copy(
            src_ref=half_ref.at[0, step, :, at],
            dst_ref=half_ref.at[1, slot, :, at],
            send_sem=half_send.at[step, chunk],
            recv_sem=half_recv.at[slot, chunk],
            device_id={"freq": (freq + step) % n_freq},
            device_id_type=mesh_ids,
        )

    piece = 512

    def pick_half(target, chunk, side, slot):
        for start in range(chunk * CHUNK, (chunk + 1) * CHUNK, piece):
            at = pl.ds(pl.multiple_of(target * segment + start, piece), piece)
            half_ref[side, slot, :, pl.ds(start, piece)] = one_hot_pick(
                gathered, arrive_ref[:, at], width
            ).astype(jnp.bfloat16)

    @pl.loop(1, n_freq)
    def _(step):
        for chunk in range(chunks):
            pick_half((freq + step) % n_freq, chunk, 0, step)
            half_copy(step, freq, chunk).start()

    for chunk in range(chunks):
        pick_half(freq, chunk, 1, freq)

    def columns(chunk):
        return pl.ds(pl.multiple_of(chunk * CHUNK, CHUNK), CHUNK)

    def result_copy(chunk):
        return pltpu.make_async_copy(
            result_ref.at[:, columns(chunk)], out_hbm.at[:, columns(chunk)], result_sem.at[chunk]
        )

    @pl.loop(0, chunks)
    def _(chunk):
        @pl.loop(1, n_freq)
        def _(step):
            half_copy(step, (freq + step) % n_freq, chunk).wait_recv()

        for group in range(n_freq):
            ordered_ref[group * SUB : (group + 1) * SUB, columns(chunk)] = half_ref[
                1, group, :, columns(chunk)
            ]
        backward_chunk(
            chunk, kind_ref, ordered_ref, first_ref, hidden_ref, last_ref, slope_ref, result_ref
        )
        result_copy(chunk).start()

    for mask in range(1, n_cells):
        far_copy(mask).wait_send()
        pass_copy(mask, core).wait_send()

    @pl.loop(1, shards)
    def _(step):
        count_copy(step, (me + step) % shards, me).wait_send()
        out_copy((me + step) % shards, me).wait_send()

    @pl.loop(1, n_freq)
    def _(step):
        for chunk in range(chunks):
            half_copy(step, freq, chunk).wait_send()

    for chunk in range(chunks):
        result_copy(chunk).wait()


def far_memory(count):
    return [pl.BlockSpec(memory_space=pltpu.HBM)] * count


def per_device(
    far_adjoint,
    wavenumber,
    design_params,
    family,
    send_pick,
    arrive_pick,
    input_weight,
    hidden_weight,
    output_weight,
):
    row_count, column_count = family.shape
    cell_count = row_count * column_count
    bands = far_adjoint.shape[0]
    band_groups = lax.axis_size("freq")
    segment = cell_count // band_groups
    chunks = segment // CHUNK
    pair_rows = 2 * bands
    shards, slots = send_pick.shape[1:]
    directions = far_adjoint.shape[1]
    n_cells = lax.axis_size("cells")
    width = 256 if slots % 256 == 0 else 128
    bf16, dma = jnp.bfloat16, pltpu.SemaphoreType.DMA
    last_weight = output_weight.reshape(NFAM, band_groups, pair_rows, HID)
    last_weight = jnp.pad(last_weight, ((0, 0), (0, 0), (0, SUB - pair_rows), (0, 0)))
    last_weight = last_weight.reshape(NFAM, band_groups * SUB, HID)
    input_weight = jnp.swapaxes(input_weight, 1, 2)
    return pl.pallas_call(
        functools.partial(fused_kernel, width=width),
        out_shape=jax.ShapeDtypeStruct(design_params.shape, jnp.float32),
        in_specs=far_memory(9),
        out_specs=pl.BlockSpec(memory_space=pltpu.HBM),
        scratch_shapes=[
            pltpu.SMEM(wavenumber.shape, jnp.float32),
            pltpu.VMEM(family.shape, jnp.int32),
            pltpu.VMEM((shards, slots), jnp.int32),
            pltpu.VMEM(arrive_pick.shape, jnp.int32),
            pltpu.VMEM(design_params.shape, bf16),
            pltpu.VMEM(input_weight.shape, bf16),
            pltpu.VMEM(hidden_weight.shape, bf16),
            pltpu.VMEM(last_weight.shape, bf16),
            dma((10,)),
            pltpu.VMEM((n_cells, bands, 2 * directions, V), bf16),
            pltpu.VMEM((bands, V, 2 * column_count), bf16),
            pltpu.VMEM((bands, 2 * row_count, 4 * U), bf16),
            pltpu.VMEM((pair_rows * row_count, column_count), bf16),
            pltpu.VMEM((row_count * SUB, column_count), bf16),
            pltpu.VMEM((shards, SUB, slots), bf16),
            pltpu.VMEM((shards, SUB, slots), bf16),
            pltpu.VMEM((shards * slots // width * SUB, width), jnp.float32),
            pltpu.VMEM((2, band_groups, SUB, segment), bf16),
            pltpu.VMEM((band_groups * SUB, segment), bf16),
            pltpu.VMEM((NFAM, 128), jnp.float32),
            pltpu.VMEM((shards, NFAM, 128), jnp.float32),
            pltpu.VMEM((1, 128), jnp.int32),
            pltpu.SMEM((1, 128), jnp.int32),
            pltpu.VMEM((NL + 1, segment, HID), bf16),
            pltpu.VMEM(design_params.shape, jnp.float32),
            dma((n_cells,)),
            dma((n_cells,)),
            dma((n_cells,)),
            dma((n_cells,)),
            dma((shards,)),
            dma((shards,)),
            dma((shards,)),
            dma((shards,)),
            dma((band_groups, chunks)),
            dma((band_groups, chunks)),
            dma((chunks,)),
        ],
        compiler_params=pltpu.CompilerParams(
            collective_id=0, has_side_effects=True, vmem_limit_bytes=62 << 20
        ),
        name="fused",
    )(
        wavenumber,
        far_adjoint.reshape(bands, 2 * directions, V),
        family,
        send_pick.reshape(shards, slots),
        arrive_pick,
        design_params,
        input_weight,
        hidden_weight,
        last_weight,
    )


def solution(mesh):
    return jax.shard_map(
        per_device,
        mesh=mesh,
        in_specs=(
            P(("groups", "freq"), "cells", None, None),
            P("freq"),
            P(None, ("groups", "cells", "freq", "rep")),
            P(("groups", "cells"), "rep"),
            P(("groups", "cells", "rep"), None, None),
            P(("groups", "cells", "rep"), None),
            P(),
            P(),
            P(),
        ),
        out_specs=P(None, ("groups", "cells", "freq", "rep")),
        check_vma=False,
    )
```

time: 37.6 us -> 35.3 us (0.939)
  Pallas kernels: 35.9 us -> 33.6 us
    pallas_call x2 -> x1, Pallas kernels: 35.9 us -> 33.6 us  [per_device(): pl.pallas_call(functools.partial(fused_kernel, width=width), out_shape=ja...]
    unnamed x0 -> x1, local copies, waits for them, and re-layouts: none -> 1.57 us
    reshape x1 -> x0, local copies, waits for them, and re-layouts: 1.51 us -> none  [per_device(): far_adjoint.reshape(bands, directions, 2 * V)]
where the time goes in v1:
time: 35.3 us; the launch traced here: 35.2 us
  Pallas kernels  33.6 us (95%)
  local copies, waits for them, and re-layouts  1.57 us (4%)
    pallas_call x1, Pallas kernels, per_device(): pl.pallas_call(functools.partial(fused_kernel, width=width), out_shape=ja...  33.6 us
    unnamed x1, local copies, waits for them, and re-layouts  1.57 us

profile of v1, /device:TPU:0, one launch (start us, length us, event | category | flops | bytes accessed | tf_op | source)
XLA Modules:
  0.0 35.2 jit_solution(15403103892418012718)
XLA Ops:
  0.0 33.6 %fused.1 = f32[8,4096]{1,0:T(8,128)} custom-call(f32[4]{0:T(128)} %wave_hbm.1, bf16[4,64,128]{2,1,0:T(8,128)(2,1)} %bitcast.3, s32[32,256]{1,0:T(8,128)} %family_hbm.1, s32[8,1536]{1,0:T(8,128)} %bitcast.4, s32[1,8192]{1,0:T(1,128)} %arrive_hbm.1, bf16[8,4096]{1,0:T(8,128)(2,1)} %inputs_hbm.1, bf16[8,8,256]{2,1,0:T(8,128)(2,1)} %bitcast.5, ...), custom_call_target="tpu_custom_call" | custom-call | tf_op jit(solution)/shard_map/fused/pallas_call | solution.py:520
  33.6 1.6 %copy.11 = f32[8,4096]{1,0:T(8,128)} copy(f32[8,4096]{1,0:T(8,128)} %fused.1) | data formatting | bytes 262144

commit v2 on v1

--- a/solution.py
+++ b/solution.py
@@ -16,7 +16,7 @@
 NFAM = 8
 SUB = 8
 CHUNK = 1024
-LATE = 1
+GRAIN = 512
 
 
 def one_hot_pick(table, index, width):
@@ -125,7 +125,7 @@
             active = preacts[place] * above
             slope_ref[level, at] = (above + active * (2.0 - above)).astype(jnp.bfloat16)
             if level < NL:
-                preacts[place] = nt_dot(active.astype(jnp.bfloat16) * half, hidden_ref[kind, level])
+                preacts[place] = nt_dot(active.astype(jnp.bfloat16), hidden_ref[kind, level])
 
 
 def backward_chunk(chunk, kind_ref, ordered_ref, first_ref, hidden_ref, last_ref, slope_ref, out_ref):
@@ -144,7 +144,7 @@
                 preferred_element_type=jnp.float32,
             )
     for place, (at, kind) in enumerate(blocks):
-        out_ref[:, at] = nt_dot(first_ref[kind], delta_of(0, place, at)) * (0.5 ** (NL + 1))
+        out_ref[:, at] = nt_dot(first_ref[kind], delta_of(0, place, at)) * 0.5
 
 
 def fused_kernel(
@@ -157,7 +157,7 @@
     first_hbm,
     hidden_hbm,
     last_hbm,
-    out_hbm,
+    result_ref,
     wave_ref,
     family_ref,
     send_ref,
@@ -182,7 +182,6 @@
     kind_vmem,
     kind_ref,
     slope_ref,
-    result_ref,
     far_send,
     far_recv,
     pass_send,
@@ -193,7 +192,6 @@
     out_recv,
     half_send,
     half_recv,
-    result_sem,
     *,
     width,
 ):
@@ -329,6 +327,11 @@
     for load in loads[2:]:
         load.wait()
 
+    @pl.loop(0, NFAM)
+    def _(kind):
+        for level in range(NL):
+            hidden_ref[kind, level] = hidden_ref[kind, level] * jnp.asarray(0.5, jnp.bfloat16)
+
     @pl.loop(1, shards)
     def _(step):
         count_copy(step, (me + step) % shards, (me + step) % shards).wait_recv()
@@ -347,17 +350,13 @@
     def forward(chunk):
         forward_chunk(chunk, kind_ref, inputs_ref, first_ref, hidden_ref, slope_ref)
 
-    early = min(chunks - LATE, n_cells - 1)
-
-    @pl.loop(1, early + 1)
-    def _(mask):
+    early, last_chunks = 1, chunks // 4
+
+    for mask in range(1, n_cells):
         far_arrival(mask).wait_recv()
         pass_copy(mask, core).start()
-        forward(mask - 1)
-
-    for mask in range(early + 1, n_cells):
-        far_arrival(mask).wait_recv()
-        pass_copy(mask, core).start()
+        if mask == 1:
+            pl.loop(0, early)(forward)
     for mask in range(1, n_cells):
         pass_copy(mask, 1 - core).wait_recv()
 
@@ -384,7 +383,7 @@
             device_id_type=mesh_ids,
         )
 
-    grain = 384
+    grain = GRAIN if slots % GRAIN == 0 else slots
 
     @pl.loop(1, shards)
     def _(step):
@@ -400,7 +399,7 @@
         picked = one_hot_pick(table_ref[...], send_ref[pl.ds(me, 1), at], column_count)
         got_ref[me, :, at] = picked.astype(jnp.bfloat16)
 
-    pl.loop(early, chunks)(forward)
+    pl.loop(early, chunks - last_chunks)(forward)
 
     @pl.loop(1, shards)
     def _(step):
@@ -445,13 +444,10 @@
     for chunk in range(chunks):
         pick_half(freq, chunk, 1, freq)
 
+    pl.loop(chunks - last_chunks, chunks)(forward)
+
     def columns(chunk):
         return pl.ds(pl.multiple_of(chunk * CHUNK, CHUNK), CHUNK)
-
-    def result_copy(chunk):
-        return pltpu.make_async_copy(
-            result_ref.at[:, columns(chunk)], out_hbm.at[:, columns(chunk)], result_sem.at[chunk]
-        )
 
     @pl.loop(0, chunks)
     def _(chunk):
@@ -466,7 +462,6 @@
         backward_chunk(
             chunk, kind_ref, ordered_ref, first_ref, hidden_ref, last_ref, slope_ref, result_ref
         )
-        result_copy(chunk).start()
 
     for mask in range(1, n_cells):
         far_copy(mask).wait_send()
@@ -481,9 +476,6 @@
     def _(step):
         for chunk in range(chunks):
             half_copy(step, freq, chunk).wait_send()
-
-    for chunk in range(chunks):
-        result_copy(chunk).wait()
 
 
 def far_memory(count):
@@ -519,9 +511,9 @@
     input_weight = jnp.swapaxes(input_weight, 1, 2)
     return pl.pallas_call(
         functools.partial(fused_kernel, width=width),
-        out_shape=jax.ShapeDtypeStruct(design_params.shape, jnp.float32),
+        out_shape=pltpu.VMEM(design_params.shape, jnp.float32),
         in_specs=far_memory(9),
-        out_specs=pl.BlockSpec(memory_space=pltpu.HBM),
+        out_specs=pl.BlockSpec(memory_space=pltpu.VMEM),
         scratch_shapes=[
             pltpu.SMEM(wavenumber.shape, jnp.float32),
             pltpu.VMEM(family.shape, jnp.int32),
@@ -547,7 +539,6 @@
             pltpu.VMEM((1, 128), jnp.int32),
             pltpu.SMEM((1, 128), jnp.int32),
             pltpu.VMEM((NL + 1, segment, HID), bf16),
-            pltpu.VMEM(design_params.shape, jnp.float32),
             dma((n_cells,)),
             dma((n_cells,)),
             dma((n_cells,)),
@@ -558,7 +549,6 @@
             dma((shards,)),
             dma((band_groups, chunks)),
             dma((band_groups, chunks)),
-            dma((chunks,)),
         ],
         compiler_params=pltpu.CompilerParams(
             collective_id=0, has_side_effects=True, vmem_limit_bytes=62 << 20

time: 35.3 us -> 31.8 us (0.901)
  Pallas kernels: 33.6 us -> 31 us
  local copies, waits for them, and re-layouts: 1.57 us -> 0.66 us
    pallas_call x1, Pallas kernels: 33.6 us -> 31 us  [per_device(): pl.pallas_call(functools.partial(fused_kernel, width=width), out_shape=pl...]
    unnamed x1, local copies, waits for them, and re-layouts: 1.57 us -> 0.66 us
where the time goes in v2:
time: 31.8 us; the launch traced here: 31.6 us
  Pallas kernels  31 us (97%)
  local copies, waits for them, and re-layouts  0.66 us (2%)
    pallas_call x1, Pallas kernels, per_device(): pl.pallas_call(functools.partial(fused_kernel, width=width), out_shape=pl...  31 us
    unnamed x1, local copies, waits for them, and re-layouts  0.66 us

profile of v2, /device:TPU:0, one launch (start us, length us, event | category | flops | bytes accessed | tf_op | source)
XLA Modules:
  0.0 31.6 jit_solution(11297594309534438834)
XLA Ops:
  0.0 31.0 %fused.1 = f32[8,4096]{1,0:T(8,128)S(1)} custom-call(f32[4]{0:T(128)} %wave_hbm.1, bf16[4,64,128]{2,1,0:T(8,128)(2,1)} %bitcast.3, s32[32,256]{1,0:T(8,128)} %family_hbm.1, s32[8,1536]{1,0:T(8,128)} %bitcast.4, s32[1,8192]{1,0:T(1,128)} %arrive_hbm.1, bf16[8,4096]{1,0:T(8,128)(2,1)} %inputs_hbm.1, bf16[8,8,256]{2,1,0:T(8,128)(2,1)} %bitcast.5, ...), custom_call_target="tpu_custom_call" | custom-call | tf_op jit(solution)/shard_map/fused/pallas_call | solution.py:512
  31.0 0.7 %copy.11 = f32[8,4096]{1,0:T(8,128)} copy(f32[8,4096]{1,0:T(8,128)S(1)} %fused.1) | data formatting | bytes 262144

commit v3 on v2

--- a/solution.py
+++ b/solution.py
@@ -17,6 +17,7 @@
 SUB = 8
 CHUNK = 1024
 GRAIN = 512
+UNROLL = 8
 
 
 def one_hot_pick(table, index, width):
@@ -123,9 +124,10 @@
         for place, (at, kind) in enumerate(blocks):
             above = 1.0 + jnp.tanh(preacts[place])
             active = preacts[place] * above
-            slope_ref[level, at] = (above + active * (2.0 - above)).astype(jnp.bfloat16)
+            above, active = above.astype(jnp.bfloat16), active.astype(jnp.bfloat16)
+            slope_ref[level, at] = above + active * (2.0 - above)
             if level < NL:
-                preacts[place] = nt_dot(active.astype(jnp.bfloat16), hidden_ref[kind, level])
+                preacts[place] = nt_dot(active, hidden_ref[kind, level])
 
 
 def backward_chunk(chunk, kind_ref, ordered_ref, first_ref, hidden_ref, last_ref, slope_ref, out_ref):
@@ -170,6 +172,7 @@
     field_ref,
     right_ref,
     left_ref,
+    image_ref,
     cells_ref,
     table_ref,
     outbox_ref,
@@ -332,6 +335,16 @@
         for level in range(NL):
             hidden_ref[kind, level] = hidden_ref[kind, level] * jnp.asarray(0.5, jnp.bfloat16)
 
+    def image_of(source):
+        for band in range(bands):
+            image = jnp.dot(
+                field_ref[source, band], right_ref[band], preferred_element_type=jnp.float32
+            ).astype(jnp.bfloat16)
+            image_ref[band, 0, source] = image[:, :column_count]
+            image_ref[band, 1, source] = image[:, column_count:]
+
+    image_of(z)
+
     @pl.loop(1, shards)
     def _(step):
         count_copy(step, (me + step) % shards, (me + step) % shards).wait_recv()
@@ -359,13 +372,10 @@
             pl.loop(0, early)(forward)
     for mask in range(1, n_cells):
         pass_copy(mask, 1 - core).wait_recv()
+        image_of(partner(z, mask, n_cells))
 
     for band in range(bands):
-        field = field_ref[:, band].reshape(2 * U, V)
-        image = jnp.dot(field, right_ref[band], preferred_element_type=jnp.float32).astype(
-            jnp.bfloat16
-        )
-        stacked = jnp.concatenate([image[:, :column_count], image[:, column_count:]], 0)
+        stacked = image_ref[band].reshape(4 * U, column_count)
         cells_ref[band * 2 * row_count : (band + 1) * 2 * row_count] = jnp.dot(
             left_ref[band], stacked, preferred_element_type=jnp.float32
         ).astype(jnp.bfloat16)
@@ -385,14 +395,19 @@
 
     grain = GRAIN if slots % GRAIN == 0 else slots
 
-    @pl.loop(1, shards)
-    def _(step):
+    def send_picked(step):
         shard = partner(me, shards - step, shards)
         for start in range(0, slots, grain):
             at = pl.ds(start, grain)
             picked = one_hot_pick(table_ref[...], send_ref[pl.ds(shard, 1), at], column_count)
             outbox_ref[shard, :, at] = picked.astype(jnp.bfloat16)
         out_copy(shard, me).start()
+
+    if shards <= UNROLL:
+        for step in range(1, shards):
+            send_picked(step)
+    else:
+        pl.loop(1, shards)(send_picked)
 
     for start in range(0, slots, grain):
         at = pl.ds(start, grain)
@@ -449,8 +464,7 @@
     def columns(chunk):
         return pl.ds(pl.multiple_of(chunk * CHUNK, CHUNK), CHUNK)
 
-    @pl.loop(0, chunks)
-    def _(chunk):
+    def backward(chunk):
         @pl.loop(1, n_freq)
         def _(step):
             half_copy(step, (freq + step) % n_freq, chunk).wait_recv()
@@ -462,6 +476,11 @@
         backward_chunk(
             chunk, kind_ref, ordered_ref, first_ref, hidden_ref, last_ref, slope_ref, result_ref
         )
+
+    @pl.loop(0, chunks // 2)
+    def _(pair):
+        backward(2 * pair)
+        backward(2 * pair + 1)
 
     for mask in range(1, n_cells):
         far_copy(mask).wait_send()
@@ -527,6 +546,7 @@
             pltpu.VMEM((n_cells, bands, 2 * directions, V), bf16),
             pltpu.VMEM((bands, V, 2 * column_count), bf16),
             pltpu.VMEM((bands, 2 * row_count, 4 * U), bf16),
+            pltpu.VMEM((bands, 2, n_cells, 2 * directions, column_count), bf16),
             pltpu.VMEM((pair_rows * row_count, column_count), bf16),
             pltpu.VMEM((row_count * SUB, column_count), bf16),
             pltpu.VMEM((shards, SUB, slots), bf16),

time: 31.8 us -> 31 us (0.975)
  Pallas kernels: 31 us -> 30.2 us
    pallas_call x1, Pallas kernels: 31 us -> 30.2 us  [per_device(): pl.pallas_call(functools.partial(fused_kernel, width=width), out_shape=pl...]
where the time goes in v3:
time: 31 us; the launch traced here: 30.9 us
  Pallas kernels  30.2 us (97%)
  local copies, waits for them, and re-layouts  0.66 us (2%)
    pallas_call x1, Pallas kernels, per_device(): pl.pallas_call(functools.partial(fused_kernel, width=width), out_shape=pl...  30.2 us
    unnamed x1, local copies, waits for them, and re-layouts  0.66 us

profile of v3, /device:TPU:0, one launch (start us, length us, event | category | flops | bytes accessed | tf_op | source)
XLA Modules:
  0.0 30.9 jit_solution(938131751724687710)
XLA Ops:
  0.0 30.2 %fused.1 = f32[8,4096]{1,0:T(8,128)S(1)} custom-call(f32[4]{0:T(128)} %wave_hbm.1, bf16[4,64,128]{2,1,0:T(8,128)(2,1)} %bitcast.3, s32[32,256]{1,0:T(8,128)} %family_hbm.1, s32[8,1536]{1,0:T(8,128)} %bitcast.4, s32[1,8192]{1,0:T(1,128)} %arrive_hbm.1, bf16[8,4096]{1,0:T(8,128)(2,1)} %inputs_hbm.1, bf16[8,8,256]{2,1,0:T(8,128)(2,1)} %bitcast.5, ...), custom_call_target="tpu_custom_call" | custom-call | tf_op jit(solution)/shard_map/fused/pallas_call | solution.py:531
  30.2 0.7 %copy.11 = f32[8,4096]{1,0:T(8,128)} copy(f32[8,4096]{1,0:T(8,128)S(1)} %fused.1) | data formatting | bytes 262144
